TPU v7x, 32 devices: a whole 2x2x4 slice. The times are simulated.
32 devices in a mesh: head: 2 (over core), seq: 16 (over z, y, x).
Axes of the slice: x: 2, y: 2, z: 4, core: 2. Of those that a mesh axis runs over, the one named last changes fastest.
Arguments:
- queries: bfloat16 [8192, 5120], P(('seq', 'head')), may hold values from -8 to 8
- key_states: bfloat16 [8192, 5120], P(('seq', 'head')), may hold values from -8 to 8
- value_states: bfloat16 [8192, 5120], P(('seq', 'head')), may hold values from -6 to 6
- cluster_perm: int32 [40, 8192], P('head', 'seq'), may hold values from 0 to 8191, as said below
- block_mask: int32 [40, 64, 64], P('head', 'seq'), may hold values from 0 to 1, as said below
Outputs:
- attention_out: bfloat16 [8192, 5120], P(('seq', 'head'))
Inputs may be any that keep to these rules, and one draw needn't show every extreme that they name: `cluster_perm`: for each head, positions k * 512 to (k + 1) * 512 - 1 list the tokens k * 512 to (k + 1) * 512 - 1, each once. `block_mask`: for each head and each aligned run of 4 query blocks, the key blocks used by some query block of the run number exactly 1. For such a run and the 20 heads g * 20 to (g + 1) * 20 - 1, the (head, key block) pairs so used that lie in one aligned run of 4 key blocks number at most 2, and exactly 2 in some run. Every query block uses 1 to 1 key blocks, and some query block of every run uses 1, for every head.
All inputs are finite; a program needn't handle non-finite values.
Results may differ from a plain program's by a relative error of at most 0.0049.
Values may be sent and summed in bfloat16 or wider, within the bound.
A program may use at most 128 MiB of HBM per device.

v0:
```python
import math
import jax
import jax.numpy as jnp
from jax import lax
from jax.sharding import PartitionSpec as P

HEAD_DIM = 128
BLOCK = 128


def shards(queries, key_states, value_states, cluster_perm, block_mask):
    group_heads = cluster_perm.shape[0]
    shard_rows = cluster_perm.shape[1]
    shard_blocks = shard_rows // BLOCK
    seq_count = lax.axis_size("seq")
    block_total = block_mask.shape[2]
    pick_count = max(1, block_total // 64)
    live_most = min(5, pick_count)
    capacity = max(
        1, min(shard_blocks, (group_heads * pick_count * 8 + 5 * seq_count - 1) // (5 * seq_count))
    )
    pair_count = group_heads * shard_blocks
    slot_total = seq_count * capacity
    score_scale = 1.0 / math.sqrt(HEAD_DIM)
    query_rows, key_rows, value_rows = (
        lax.all_to_all(queries, "head", split_axis=1, concat_axis=0, tiled=True),
        lax.all_to_all(key_states, "head", split_axis=1, concat_axis=0, tiled=True),
        lax.all_to_all(value_states, "head", split_axis=1, concat_axis=0, tiled=True),
    )
    local_perm = cluster_perm - lax.axis_index("seq") * shard_rows
    row_ids = jnp.arange(shard_rows, dtype=jnp.int32)
    order_table = (local_perm[:, :, None] == row_ids[None, None, :]).astype(jnp.bfloat16)
    stacked = jnp.concatenate(
        [
            query_rows.reshape(shard_rows, group_heads, HEAD_DIM),
            key_rows.reshape(shard_rows, group_heads, HEAD_DIM),
            value_rows.reshape(shard_rows, group_heads, HEAD_DIM),
        ],
        axis=2,
    )
    sorted_all = jnp.einsum(
        "hit,thd->hid", order_table, stacked, preferred_element_type=jnp.float32
    ).astype(jnp.bfloat16)
    query_sorted = sorted_all[:, :, :HEAD_DIM]
    key_sorted = sorted_all[:, :, HEAD_DIM : 2 * HEAD_DIM]
    value_sorted = sorted_all[:, :, 2 * HEAD_DIM :]
    needed = jnp.max(block_mask, axis=1)
    by_owner = needed.reshape(group_heads, seq_count, shard_blocks)
    requested = lax.all_to_all(by_owner, "seq", split_axis=1, concat_axis=1, tiled=True)

    def slot_ranks(bit_table):
        flat_bits = bit_table.transpose(1, 0, 2).reshape(seq_count, pair_count)
        return (flat_bits, jnp.cumsum(flat_bits, axis=1) - flat_bits)

    asked_bits, asked_rank = slot_ranks(requested)
    cap_ids = jnp.arange(capacity, dtype=jnp.int32)
    matches = (asked_bits[:, :, None] == 1) & (asked_rank[:, :, None] == cap_ids[None, None, :])
    send_table = matches.transpose(0, 2, 1).astype(jnp.bfloat16)
    block_width = BLOCK * HEAD_DIM
    kv_pairs = jnp.concatenate(
        [
            key_sorted.reshape(pair_count, block_width),
            value_sorted.reshape(pair_count, block_width),
        ],
        axis=1,
    )
    kv_send = jnp.einsum(
        "scp,pw->scw", send_table, kv_pairs, preferred_element_type=jnp.float32
    ).astype(jnp.bfloat16)
    key_send = kv_send[:, :, :block_width].reshape(seq_count, capacity, BLOCK, HEAD_DIM)
    value_send = kv_send[:, :, block_width:].reshape(seq_count, capacity, BLOCK, HEAD_DIM)
    own_bits, own_rank = slot_ranks(by_owner)
    prefix = jnp.cumsum(needed, axis=1) - needed
    chosen = (needed[:, :, None] == 1) & (
        prefix[:, :, None] == jnp.arange(pick_count, dtype=jnp.int32)[None, None, :]
    )
    picked = jnp.sum(
        jnp.where(chosen, jnp.arange(block_total, dtype=jnp.int32)[None, :, None], 0), axis=1
    )
    owner_idx = picked // shard_blocks
    pair_idx = (
        jnp.arange(group_heads, dtype=jnp.int32)[:, None] * shard_blocks + picked % shard_blocks
    )
    slot_idx = jnp.take(own_rank.reshape(-1), owner_idx * pair_count + pair_idx)
    position = owner_idx * capacity + slot_idx
    live_bits = jnp.take_along_axis(block_mask, picked[:, None, :], axis=2)
    query_blocks = query_sorted.reshape(group_heads, shard_blocks, BLOCK, HEAD_DIM)
    rank_live = jnp.cumsum(live_bits, axis=2) - live_bits
    selected = (live_bits[..., None] == 1) & (
        rank_live[..., None] == jnp.arange(live_most, dtype=jnp.int32)
    )
    which_pick = jnp.sum(
        jnp.where(selected, jnp.arange(pick_count, dtype=jnp.int32)[None, None, :, None], 0), axis=2
    )
    usable = jnp.any(selected, axis=2)
    key_pos = jnp.take_along_axis(
        jnp.broadcast_to(position[:, None, :], live_bits.shape), which_pick, axis=2
    )
    score_form = "qid,qljd->qilj"
    mix_form = "qilj,qljd->qid"
    slot_ids = jnp.arange(slot_total, dtype=jnp.int32)

    def select_blocks(got_flat, slot_head):
        pick_table = (slot_head[..., None] == slot_ids).astype(jnp.bfloat16)
        chosen_rows = jnp.einsum(
            "...s,sw->...w", pick_table, got_flat, preferred_element_type=jnp.float32
        ).astype(jnp.bfloat16)
        return chosen_rows.reshape(slot_head.shape + (BLOCK, HEAD_DIM))

    def head_scores(query_head, key_got, slot_head, usable_head):
        key_sel = select_blocks(key_got, slot_head)
        scores = (
            jnp.einsum(score_form, query_head, key_sel, preferred_element_type=jnp.float32)
            * score_scale
        )
        return jnp.where(usable_head[:, None, :, None], scores, -jnp.inf)

    def head_mix(weights, value_got, slot_head):
        value_sel = select_blocks(value_got, slot_head)
        return jnp.einsum(mix_form, weights, value_sel, preferred_element_type=jnp.float32).astype(
            jnp.bfloat16
        )

    flat_shape = (slot_total, block_width)
    key_got, value_got = (
        lax.all_to_all(key_send, "seq", split_axis=0, concat_axis=0, tiled=True),
        lax.all_to_all(value_send, "seq", split_axis=0, concat_axis=0, tiled=True),
    )
    key_got = key_got.reshape(flat_shape)
    value_got = value_got.reshape(flat_shape)

    def full_pass(operands):
        query_head, slot_head, usable_head = operands
        scores = head_scores(query_head, key_got, slot_head, usable_head)
        row_top = jnp.max(scores, axis=(2, 3), keepdims=True)
        exponent = jnp.exp(scores - row_top)
        row_total = jnp.sum(exponent, axis=(2, 3), keepdims=True)
        weights = (exponent / row_total).astype(jnp.bfloat16)
        return head_mix(weights, value_got, slot_head)

    attended = lax.map(full_pass, (query_blocks, key_pos, usable))
    attended_flat = attended.reshape(group_heads, shard_rows, HEAD_DIM)
    restored = jnp.einsum(
        "hit,hid->thd", order_table, attended_flat, preferred_element_type=jnp.float32
    ).astype(jnp.bfloat16)
    out_rows = restored.reshape(shard_rows, group_heads * HEAD_DIM)
    return lax.all_to_all(out_rows, "head", split_axis=0, concat_axis=1, tiled=True)


def solution(mesh):
    placed = (
        P(("seq", "head"), None),
        P(("seq", "head"), None),
        P(("seq", "head"), None),
        P("head", "seq"),
        P("head", "seq", None),
    )
    return jax.shard_map(
        shards, mesh=mesh, in_specs=placed, out_specs=P(("seq", "head"), None), check_vma=False
    )
```

profile of v0, /device:TPU:9, one launch (start us, length us, event | category | flops | bytes accessed | tf_op | source)
XLA Modules:
  0.0 287.1 jit_solution(12030051631349020649)
XLA Ops:
  0.0 4.4 %copy.43 = bf16[256,5120]{0,1:T(8,128)(2,1)} copy(bf16[256,5120]{1,0:T(8,128)(2,1)} %param.7) | data formatting | bytes 5242880 | tf_op args[0]
  4.4 4.7 %all-to-all-start = ((bf16[256,2,2560]{0,2,1:T(8,128)(2,1)}), bf16[256,2,2560]{0,2,1:T(8,128)(2,1)S(1)}, u32[]{:S(2)}, u32[]{:S(2)}) async-start(bf16[256,2,2560]{0,2,1:T(8,128)(2,1)} %bitcast.147), calls=%async_computation | async-start | bytes 5242880 | tf_op jit(solution)/shard_map/all_to_all | solution.py:26
  9.8 4.4 %copy.45 = bf16[256,5120]{0,1:T(8,128)(2,1)} copy(bf16[256,5120]{1,0:T(8,128)(2,1)} %param.8) | data formatting | bytes 5242880 | tf_op args[1]
  14.2 5.0 %all-to-all-start.1 = ((bf16[256,2,2560]{0,2,1:T(8,128)(2,1)}), bf16[256,2,2560]{0,2,1:T(8,128)(2,1)}, u32[]{:S(2)}, u32[]{:S(2)}) async-start(bf16[256,2,2560]{0,2,1:T(8,128)(2,1)} %bitcast.145), calls=%async_computation.1 | async-start | bytes 5242880 | tf_op jit(solution)/shard_map/all_to_all | solution.py:27
  19.2 17.3 %copy.44 = bf16[2,256,2560]{1,0,2:T(2,128)(2,1)} copy(bf16[2,256,2560]{1,2,0:T(8,128)(2,1)S(1)} %bitcast.143) | data formatting | bytes 5242880 | tf_op jit(solution)/shard_map/all_to_all | solution.py:26
  36.5 4.2 %reshape.468 = bf16[512,20,128]{0,2,1:T(8,128)(2,1)S(1)} reshape(bf16[2,256,2560]{1,0,2:T(2,128)(2,1)} %copy.44) | data formatting | bytes 5242880 | tf_op jit(solution)/shard_map/reshape | solution.py:35
  43.2 4.4 %copy.47 = bf16[256,5120]{0,1:T(8,128)(2,1)} copy(bf16[256,5120]{1,0:T(8,128)(2,1)} %param.9) | data formatting | bytes 5242880 | tf_op args[2]
  47.6 3.9 %all-to-all-start.2 = ((bf16[256,2,2560]{0,2,1:T(8,128)(2,1)}), bf16[256,2,2560]{0,2,1:T(8,128)(2,1)S(1)}, u32[]{:S(2)}, u32[]{:S(2)}) async-start(bf16[256,2,2560]{0,2,1:T(8,128)(2,1)} %bitcast.146), calls=%async_computation.2 | async-start | bytes 5242880 | tf_op jit(solution)/shard_map/all_to_all | solution.py:28
  51.5 7.0 %copy.46 = bf16[2,256,2560]{1,0,2:T(2,128)(2,1)} copy(bf16[2,256,2560]{1,2,0:T(8,128)(2,1)} %bitcast.7) | data formatting | bytes 5242880 | tf_op jit(solution)/shard_map/all_to_all | solution.py:27
  58.4 5.4 %reshape.469 = bf16[512,20,128]{0,2,1:T(8,128)(2,1)} reshape(bf16[2,256,2560]{1,0,2:T(2,128)(2,1)} %copy.46) | data formatting | bytes 5242880 | tf_op jit(solution)/shard_map/reshape | solution.py:36
  63.8 4.4 %copy.50 = bf16[512,20,128]{2,0,1:T(8,128)(2,1)} copy(bf16[512,20,128]{0,2,1:T(8,128)(2,1)} %reshape.469) | data formatting | bytes 5242880 | tf_op jit(solution)/shard_map/reshape | solution.py:36
  68.2 6.7 %all-to-all-start.3 = ((s32[20,16,4]{0,2,1:T(4,128)}), s32[20,16,4]{0,2,1:T(4,128)S(1)}, u32[]{:S(2)}, u32[]{:S(2)}) async-start(s32[20,16,4]{0,2,1:T(4,128)} %bitcast.11), calls=%async_computation.3 | async-start | bytes 65536 | tf_op jit(solution)/shard_map/all_to_all | solution.py:49
  74.9 17.3 %copy.48 = bf16[2,256,2560]{1,0,2:T(2,128)(2,1)} copy(bf16[2,256,2560]{1,2,0:T(8,128)(2,1)S(1)} %bitcast.144) | data formatting | bytes 5242880 | tf_op jit(solution)/shard_map/all_to_all | solution.py:28
  92.2 4.2 %reshape.470 = bf16[512,20,128]{0,2,1:T(8,128)(2,1)S(1)} reshape(bf16[2,256,2560]{1,0,2:T(2,128)(2,1)} %copy.48) | data formatting | bytes 5242880 | tf_op jit(solution)/shard_map/reshape | solution.py:37
  98.9 7.9 %fusion.39 = bf16[20,512,384]{2,1,0:T(8,128)(2,1)S(1)} fusion(bf16[512,20,128]{2,0,1:T(8,128)(2,1)} %copy.51, bf16[512,20,128]{2,0,1:T(8,128)(2,1)} %copy.50, bf16[512,20,128]{2,0,1:T(8,128)(2,1)} %copy.49, s32[20,512]{1,0:T(8,128)S(1)} %broadcast_subtract_fusion), kind=kOutput, calls=%fused_computation.46 | convolution fusion | flops 4059299840 | bytes 15769600 | tf_op jit(solution)/shard_map/hit,thd->hid/dot_general | solution.py:41
  109.9 5.2 %reshape.475 = bf16[80,16384]{1,0:T(8,128)(2,1)} reshape(bf16[20,512,128]{2,1,0:T(8,128)(2,1)} %get-tuple-element.99) | data formatting | bytes 5242880 | tf_op jit(solution)/shard_map/reshape | solution.py:62
  123.5 6.4 %all-to-all-start.4 = ((bf16[16,2,128,128]{3,2,1,0:T(8,128)(2,1)}), bf16[16,2,128,128]{3,2,1,0:T(8,128)(2,1)S(1)}, u32[]{:S(2)}, u32[]{:S(2)}) async-start(bf16[16,2,128,128]{3,2,1,0:T(8,128)(2,1)} %copy.61), calls=%async_computation.4 | async-start | bytes 2097152 | tf_op jit(solution)/shard_map/all_to_all | solution.py:126
  131.1 23.1 %all-to-all-done.4 = bf16[16,2,128,128]{3,2,1,0:T(8,128)(2,1)S(1)} async-done(((bf16[16,2,128,128]{3,2,1,0:T(8,128)(2,1)}), bf16[16,2,128,128]{3,2,1,0:T(8,128)(2,1)S(1)}, u32[]{:S(2)}, u32[]{:S(2)}) %all-to-all-start.4) | async-done | bytes 1048608 | tf_op jit(solution)/shard_map/all_to_all | solution.py:126
  154.2 4.5 %all-to-all-start.5 = ((bf16[16,2,128,128]{3,2,1,0:T(8,128)(2,1)}), bf16[16,2,128,128]{3,2,1,0:T(8,128)(2,1)S(1)}, u32[]{:S(2)}, u32[]{:S(2)}) async-start(bf16[16,2,128,128]{3,2,1,0:T(8,128)(2,1)} %copy.62), calls=%async_computation.5 | async-start | bytes 2097152 | tf_op jit(solution)/shard_map/all_to_all | solution.py:127
  166.4 16.7 %all-to-all-done.5 = bf16[16,2,128,128]{3,2,1,0:T(8,128)(2,1)S(1)} async-done(((bf16[16,2,128,128]{3,2,1,0:T(8,128)(2,1)}), bf16[16,2,128,128]{3,2,1,0:T(8,128)(2,1)S(1)}, u32[]{:S(2)}, u32[]{:S(2)}) %all-to-all-start.5) | async-done | bytes 1048608 | tf_op jit(solution)/shard_map/all_to_all | solution.py:127
  183.8 81.5 %while.11 = (s32[]{:T(128)}, bf16[20,4,128,128]{3,2,1,0:T(8,128)(2,1)}, pred[20,4,1]{0,1,2:T(4,128)(4,1)S(1)}, bf16[20,4,128,128]{3,2,1,0:T(8,128)(2,1)}, s32[20...) while((s32[]{:T(128)}, ...), condition=%wide.region_8.9_spmd.clone, body=%wide.region_5.8_spmd.clone.sunk | while | flops 59507712 | bytes 3936457 | solution.py:141
  265.4 7.2 %convert_bitcast_fusion = bf16[512,20,128]{0,2,1:T(8,128)(2,1)} fusion(bf16[20,512,128]{2,1,0:T(8,128)(2,1)} %bitcast.162, s32[20,512]{1,0:T(8,128)S(1)} %broadcast_subtract_fusion), kind=kOutput, calls=%fused_computation.50 | convolution fusion | flops 1348730880 | bytes 5283840 | tf_op jit(solution)/shard_map/hit,hid->thd/dot_general | solution.py:143
  272.6 3.5 %all_to_all.71 = bf16[2,256,2560]{1,0,2:T(2,128)(2,1)S(1)} reshape(bf16[512,20,128]{0,2,1:T(8,128)(2,1)} %convert_bitcast_fusion) | data formatting | bytes 5242880 | tf_op jit(solution)/shard_map/all_to_all | solution.py:147
  276.5 7.9 %all_to_all.82 = bf16[2,256,2560]{1,2,0:T(8,128)(2,1)S(1)} all-to-all(bf16[2,256,2560]{1,2,0:T(8,128)(2,1)S(1)} %copy.66), channel_id=1, replica_groups=mesh['head'=2,'seq'=16] {'head'}, dimensions={0} | all-to-all | bytes 5242880 | tf_op jit(solution)/shard_map/all_to_all | solution.py:147
  (223 shorter events, 111.2 us)
Async XLA Ops:
  4.4 4.7 %copy-start = (s32[20,4,64]{2,1,0:T(4,128)S(1)}, s32[20,4,64]{2,1,0:T(4,128)}, u32[]{:S(2)}) copy-start(s32[20,4,64]{2,1,0:T(4,128)} %param.11) | copy-start | bytes 61444
  4.4 9.8 %all-to-all-start = ((bf16[256,2,2560]{0,2,1:T(8,128)(2,1)}), bf16[256,2,2560]{0,2,1:T(8,128)(2,1)S(1)}, u32[]{:S(2)}, u32[]{:S(2)}) async-start(bf16[256,2,2560]{0,2,1:T(8,128)(2,1)} %bitcast.147), calls=%async_computation | async-start | bytes 5242880 | tf_op jit(solution)/shard_map/all_to_all | solution.py:26
  14.2 33.4 %all-to-all-start.1 = ((bf16[256,2,2560]{0,2,1:T(8,128)(2,1)}), bf16[256,2,2560]{0,2,1:T(8,128)(2,1)}, u32[]{:S(2)}, u32[]{:S(2)}) async-start(bf16[256,2,2560]{0,2,1:T(8,128)(2,1)} %bitcast.145), calls=%async_computation.1 | async-start | bytes 5242880 | tf_op jit(solution)/shard_map/all_to_all | solution.py:27
  47.6 20.6 %all-to-all-start.2 = ((bf16[256,2,2560]{0,2,1:T(8,128)(2,1)}), bf16[256,2,2560]{0,2,1:T(8,128)(2,1)S(1)}, u32[]{:S(2)}, u32[]{:S(2)}) async-start(bf16[256,2,2560]{0,2,1:T(8,128)(2,1)} %bitcast.146), calls=%async_computation.2 | async-start | bytes 5242880 | tf_op jit(solution)/shard_map/all_to_all | solution.py:28
  68.2 49.9 %all-to-all-start.3 = ((s32[20,16,4]{0,2,1:T(4,128)}), s32[20,16,4]{0,2,1:T(4,128)S(1)}, u32[]{:S(2)}, u32[]{:S(2)}) async-start(s32[20,16,4]{0,2,1:T(4,128)} %bitcast.11), calls=%async_computation.3 | async-start | bytes 65536 | tf_op jit(solution)/shard_map/all_to_all | solution.py:49
  96.3 2.6 copy-start.1
  123.5 30.7 %all-to-all-start.4 = ((bf16[16,2,128,128]{3,2,1,0:T(8,128)(2,1)}), bf16[16,2,128,128]{3,2,1,0:T(8,128)(2,1)S(1)}, u32[]{:S(2)}, u32[]{:S(2)}) async-start(bf16[16,2,128,128]{3,2,1,0:T(8,128)(2,1)} %copy.61), calls=%async_computation.4 | async-start | bytes 2097152 | tf_op jit(solution)/shard_map/all_to_all | solution.py:126
  154.2 28.9 %all-to-all-start.5 = ((bf16[16,2,128,128]{3,2,1,0:T(8,128)(2,1)}), bf16[16,2,128,128]{3,2,1,0:T(8,128)(2,1)S(1)}, u32[]{:S(2)}, u32[]{:S(2)}) async-start(bf16[16,2,128,128]{3,2,1,0:T(8,128)(2,1)} %copy.62), calls=%async_computation.5 | async-start | bytes 2097152 | tf_op jit(solution)/shard_map/all_to_all | solution.py:127
where the time goes:
time: 290 us; the launch traced here: 287 us
  local copies, waits for them, and re-layouts  111 us (38%)
  matrix products  95.6 us (33%)
  waiting for transfers between devices  39.8 us (14%)
  starting transfers between devices  31.2 us (11%)
  blocking collectives  7.86 us (3%)
    sub x20, matrix products, full_pass(): exponent = jnp.exp(scores - row_top)  23.4 us
    all_to_all x1, waiting for transfers between devices, shards(): lax.all_to_all(key_send, 'seq', split_axis=0, concat_axis=0, tiled=True)  23.1 us
    dot_general x20, matrix products, head_scores(): jnp.einsum(score_form, query_head, key_sel, preferred_element_type=jnp.fl...  22.3 us
    dot_general x20, matrix products, head_mix(): jnp.einsum(mix_form, weights, value_sel, preferred_element_type=jnp.float32)  18.7 us
    all_to_all x1, local copies, waits for them, and re-layouts, shards(): lax.all_to_all(value_states, 'head', split_axis=1, concat_axis=0, tiled=T...  17.3 us
    all_to_all x1, local copies, waits for them, and re-layouts, shards(): lax.all_to_all(queries, 'head', split_axis=1, concat_axis=0, tiled=True)  17.3 us
    all_to_all x1, waiting for transfers between devices, shards(): lax.all_to_all(value_send, 'seq', split_axis=0, concat_axis=0, tiled=True)  16.7 us
    unnamed x15, local copies, waits for them, and re-layouts  15.3 us
  transfers between devices with their start and end apart: 6, of which 2 were waited for; matrix products, arithmetic and copies ran while one was open for 36% of the time, Pallas kernels for 0%

commit v1 on v0

--- a/solution.py
+++ b/solution.py
@@ -23,7 +23,12 @@
     slot_total = seq_count * capacity
     score_scale = 1.0 / math.sqrt(HEAD_DIM)
     query_rows, key_rows, value_rows = (
-        lax.all_to_all(queries, "head", split_axis=1, concat_axis=0, tiled=True),
+        jnp.concatenate(
+            lax.all_to_all(
+                jnp.stack(jnp.split(queries, lax.axis_size("head"), axis=1)), "head", 0, 0
+            ),
+            axis=0,
+        ),
         lax.all_to_all(key_states, "head", split_axis=1, concat_axis=0, tiled=True),
         lax.all_to_all(value_states, "head", split_axis=1, concat_axis=0, tiled=True),
     )

time: 290 us -> 272 us (0.938)
  local copies, waits for them, and re-layouts: 111 us -> 92.4 us
    all_to_all x1 -> x0, local copies, waits for them, and re-layouts: 17.3 us -> none  [shards(): lax.all_to_all(queries, 'head', split_axis=1, concat_axis=0, tiled=True)]
    another operation x0 -> x3, local copies, waits for them, and re-layouts: none -> 8.13 us  [the longest x2 6.25 us: shards(): query_rows.reshape(shard_rows, group_heads, HEAD_DIM)]
    reshape x2 -> x0, local copies, waits for them, and re-layouts: 6.74 us -> none  [shards(): query_rows.reshape(shard_rows, group_heads, HEAD_DIM)]
    all_to_all x1, waiting for transfers between devices: 16.7 us -> 23.1 us  [shards(): lax.all_to_all(value_send, 'seq', split_axis=0, concat_axis=0, tiled=True)]
    all_to_all x1, waiting for transfers between devices: 23.1 us -> 16.7 us  [shards(): lax.all_to_all(key_send, 'seq', split_axis=0, concat_axis=0, tiled=True)]
    unnamed x15 -> x16, local copies, waits for them, and re-layouts: 15.3 us -> 12.4 us
  transfers between devices with their start and end apart: 6 -> 6, of which waited for: 2 -> 2; matrix products, arithmetic and copies ran while one was open for 36% -> 31% of each run, Pallas kernels for 0% -> 0%
where the time goes in v1:
time: 272 us; the launch traced here: 270 us
  matrix products  95.6 us (35%)
  local copies, waits for them, and re-layouts  92.4 us (34%)
  waiting for transfers between devices  39.8 us (15%)
  starting transfers between devices  31.1 us (11%)
  blocking collectives  7.86 us (3%)
  other arithmetic  2.78 us (1%)
    sub x20, matrix products, full_pass(): exponent = jnp.exp(scores - row_top)  23.4 us
    all_to_all x1, waiting for transfers between devices, shards(): lax.all_to_all(value_send, 'seq', split_axis=0, concat_axis=0, tiled=True)  23.1 us
    dot_general x20, matrix products, head_scores(): jnp.einsum(score_form, query_head, key_sel, preferred_element_type=jnp.fl...  22.2 us
    dot_general x20, matrix products, head_mix(): jnp.einsum(mix_form, weights, value_sel, preferred_element_type=jnp.float32)  18.7 us
    all_to_all x1, local copies, waits for them, and re-layouts, shards(): lax.all_to_all(value_states, 'head', split_axis=1, concat_axis=0, tiled=T...  17.3 us
    all_to_all x1, waiting for transfers between devices, shards(): lax.all_to_all(key_send, 'seq', split_axis=0, concat_axis=0, tiled=True)  16.7 us
    dot_general x40, matrix products, select_blocks(): jnp.einsum('...s,sw->...w', pick_table, got_flat, preferred_element_type=...  12.8 us
    unnamed x16, local copies, waits for them, and re-layouts  12.4 us
  transfers between devices with their start and end apart: 6, of which 2 were waited for; matrix products, arithmetic and copies ran while one was open for 31% of the time, Pallas kernels for 0%

profile of v1, /device:TPU:9, one launch (start us, length us, event | category | flops | bytes accessed | tf_op | source)
XLA Modules:
  0.0 270.1 jit_solution(4986914976146314200)
XLA Ops:
  3.6 4.7 %all-to-all-start = ((bf16[2,256,2560]{2,1,0:T(8,128)(2,1)}), bf16[2,256,2560]{2,1,0:T(8,128)(2,1)S(1)}, u32[]{:S(2)}, u32[]{:S(2)}) async-start(bf16[2,256,2560]{2,1,0:T(8,128)(2,1)} %pad_maximum_fusion), calls=%async_computation | async-start | bytes 5242880 | tf_op jit(solution)/shard_map/all_to_all | solution.py:27
  9.0 4.4 %copy.44 = bf16[256,5120]{0,1:T(8,128)(2,1)} copy(bf16[256,5120]{1,0:T(8,128)(2,1)} %param.8) | data formatting | bytes 5242880 | tf_op args[1]
  14.9 5.0 %all-to-all-start.1 = ((bf16[256,2,2560]{0,2,1:T(8,128)(2,1)}), bf16[256,2,2560]{0,2,1:T(8,128)(2,1)}, u32[]{:S(2)}, u32[]{:S(2)}) async-start(bf16[256,2,2560]{0,2,1:T(8,128)(2,1)} %bitcast.144), calls=%async_computation.1 | async-start | bytes 5242880 | tf_op jit(solution)/shard_map/all_to_all | solution.py:32
  19.9 4.2 %reshape.503 = bf16[512,20,128]{2,1,0:T(8,128)(2,1)S(1)} reshape(bf16[2,256,2560]{2,1,0:T(8,128)(2,1)} %copy-done) | data formatting | bytes 5242880 | tf_op jit(solution)/shard_map/reshape;reshape | solution.py:40
  26.2 4.4 %copy.46 = bf16[256,5120]{0,1:T(8,128)(2,1)} copy(bf16[256,5120]{1,0:T(8,128)(2,1)} %param.9) | data formatting | bytes 5242880 | tf_op args[2]
  30.6 3.9 %all-to-all-start.2 = ((bf16[256,2,2560]{0,2,1:T(8,128)(2,1)}), bf16[256,2,2560]{0,2,1:T(8,128)(2,1)S(1)}, u32[]{:S(2)}, u32[]{:S(2)}) async-start(bf16[256,2,2560]{0,2,1:T(8,128)(2,1)} %bitcast.145), calls=%async_computation.2 | async-start | bytes 5242880 | tf_op jit(solution)/shard_map/all_to_all | solution.py:33
  34.4 7.0 %copy.45 = bf16[2,256,2560]{1,0,2:T(2,128)(2,1)} copy(bf16[2,256,2560]{1,2,0:T(8,128)(2,1)} %bitcast.7) | data formatting | bytes 5242880 | tf_op jit(solution)/shard_map/all_to_all | solution.py:32
  41.4 5.4 %reshape.461 = bf16[512,20,128]{0,2,1:T(8,128)(2,1)} reshape(bf16[2,256,2560]{1,0,2:T(2,128)(2,1)} %copy.45) | data formatting | bytes 5242880 | tf_op jit(solution)/shard_map/reshape | solution.py:41
  46.8 4.4 %copy.49 = bf16[512,20,128]{2,0,1:T(8,128)(2,1)} copy(bf16[512,20,128]{0,2,1:T(8,128)(2,1)} %reshape.461) | data formatting | bytes 5242880 | tf_op jit(solution)/shard_map/reshape | solution.py:41
  51.2 6.7 %all-to-all-start.3 = ((s32[20,16,4]{0,2,1:T(4,128)}), s32[20,16,4]{0,2,1:T(4,128)S(1)}, u32[]{:S(2)}, u32[]{:S(2)}) async-start(s32[20,16,4]{0,2,1:T(4,128)} %bitcast.11), calls=%async_computation.3 | async-start | bytes 65536 | tf_op jit(solution)/shard_map/all_to_all | solution.py:54
  57.8 17.3 %copy.47 = bf16[2,256,2560]{1,0,2:T(2,128)(2,1)} copy(bf16[2,256,2560]{1,2,0:T(8,128)(2,1)S(1)} %bitcast.143) | data formatting | bytes 5242880 | tf_op jit(solution)/shard_map/all_to_all | solution.py:33
  75.1 4.2 %reshape.462 = bf16[512,20,128]{0,2,1:T(8,128)(2,1)S(1)} reshape(bf16[2,256,2560]{1,0,2:T(2,128)(2,1)} %copy.47) | data formatting | bytes 5242880 | tf_op jit(solution)/shard_map/reshape | solution.py:42
  81.9 7.9 %fusion.39 = bf16[20,512,384]{2,1,0:T(8,128)(2,1)S(1)} fusion(bf16[512,20,128]{2,0,1:T(8,128)(2,1)} %copy.50, bf16[512,20,128]{2,0,1:T(8,128)(2,1)} %copy.49, bf16[512,20,128]{2,0,1:T(8,128)(2,1)} %copy.48, s32[20,512]{1,0:T(8,128)S(1)} %broadcast_subtract_fusion), kind=kOutput, calls=%fused_computation.46 | convolution fusion | flops 4059299840 | bytes 15769600 | tf_op jit(solution)/shard_map/hit,thd->hid/dot_general | solution.py:46
  89.7 3.1 %fusion.68 = (bf16[20,512,128]{2,1,0:T(8,128)(2,1)}, bf16[20,512,128]{2,1,0:T(8,128)(2,1)S(1)}, bf16[20,512,128]{2,1,0:T(8,128)(2,1)}) fusion(bf16[20,512,384]{2,1,0:T(8,128)(2,1)S(1)} %fusion.39), kind=kLoop, calls=%fused_computation.105 | loop fusion | bytes 15728640 | tf_op jit(solution)/shard_map/slice | solution.py:50
  92.8 5.2 %reshape.467 = bf16[80,16384]{1,0:T(8,128)(2,1)} reshape(bf16[20,512,128]{2,1,0:T(8,128)(2,1)} %get-tuple-element.99) | data formatting | bytes 5242880 | tf_op jit(solution)/shard_map/reshape | solution.py:67
  101.6 3.4 %convolution_convert_fusion.3 = bf16[16,2,32768]{2,0,1:T(8,128)(2,1)S(1)} fusion(bf16[80,16384]{1,0:T(8,128)(2,1)} %reshape.468, bf16[80,16384]{1,0:T(8,128)(2,1)} %reshape.467, s32[16,80]{1,0:T(8,128)S(1)} %sub.46, pred[16,80]{1,0:T(8,128)(4,1)S(1)} %copy.57), kind=kOutput, calls=%fused_computation.35 | convolution fusion | flops 179311616 | bytes 7346432 | tf_op jit(solution)/shard_map/scp,pw->scw/dot_general | solution.py:72
  106.4 6.4 %all-to-all-start.5 = ((bf16[16,2,128,128]{3,2,1,0:T(8,128)(2,1)}), bf16[16,2,128,128]{3,2,1,0:T(8,128)(2,1)S(1)}, u32[]{:S(2)}, u32[]{:S(2)}) async-start(bf16[16,2,128,128]{3,2,1,0:T(8,128)(2,1)} %copy.61), calls=%async_computation.5 | async-start | bytes 2097152 | tf_op jit(solution)/shard_map/all_to_all | solution.py:132
  114.1 23.1 %all-to-all-done.5 = bf16[16,2,128,128]{3,2,1,0:T(8,128)(2,1)S(1)} async-done(((bf16[16,2,128,128]{3,2,1,0:T(8,128)(2,1)}), bf16[16,2,128,128]{3,2,1,0:T(8,128)(2,1)S(1)}, u32[]{:S(2)}, u32[]{:S(2)}) %all-to-all-start.5) | async-done | bytes 1048608 | tf_op jit(solution)/shard_map/all_to_all | solution.py:132
  137.2 4.6 %all-to-all-start.4 = ((bf16[16,2,128,128]{3,2,1,0:T(8,128)(2,1)}), bf16[16,2,128,128]{3,2,1,0:T(8,128)(2,1)S(1)}, u32[]{:S(2)}, u32[]{:S(2)}) async-start(bf16[16,2,128,128]{3,2,1,0:T(8,128)(2,1)} %copy.60), calls=%async_computation.4 | async-start | bytes 2097152 | tf_op jit(solution)/shard_map/all_to_all | solution.py:131
  149.4 16.7 %all-to-all-done.4 = bf16[16,2,128,128]{3,2,1,0:T(8,128)(2,1)S(1)} async-done(((bf16[16,2,128,128]{3,2,1,0:T(8,128)(2,1)}), bf16[16,2,128,128]{3,2,1,0:T(8,128)(2,1)S(1)}, u32[]{:S(2)}, u32[]{:S(2)}) %all-to-all-start.4) | async-done | bytes 1048608 | tf_op jit(solution)/shard_map/all_to_all | solution.py:131
  166.8 81.6 %while.11 = (s32[]{:T(128)}, bf16[20,4,128,128]{3,2,1,0:T(8,128)(2,1)}, pred[20,4,1]{0,1,2:T(4,128)(4,1)S(1)}, bf16[20,4,128,128]{3,2,1,0:T(8,128)(2,1)}, s32[20...) while((s32[]{:T(128)}, ...), condition=%wide.region_8.9_spmd.clone, body=%wide.region_5.8_spmd.clone.sunk | while | flops 59507712 | bytes 3937973 | solution.py:146
  248.4 7.2 %convert_bitcast_fusion = bf16[512,20,128]{0,2,1:T(8,128)(2,1)} fusion(bf16[20,512,128]{2,1,0:T(8,128)(2,1)} %bitcast.160, s32[20,512]{1,0:T(8,128)S(1)} %broadcast_subtract_fusion), kind=kOutput, calls=%fused_computation.51 | convolution fusion | flops 1348730880 | bytes 5283840 | tf_op jit(solution)/shard_map/hit,hid->thd/dot_general | solution.py:148
  255.6 3.5 %all_to_all.60 = bf16[2,256,2560]{1,0,2:T(2,128)(2,1)S(1)} reshape(bf16[512,20,128]{0,2,1:T(8,128)(2,1)} %convert_bitcast_fusion) | data formatting | bytes 5242880 | tf_op jit(solution)/shard_map/all_to_all | solution.py:152
  259.5 7.9 %all_to_all.71 = bf16[2,256,2560]{1,2,0:T(8,128)(2,1)S(1)} all-to-all(bf16[2,256,2560]{1,2,0:T(8,128)(2,1)S(1)} %copy.65), channel_id=1, replica_groups=mesh['head'=2,'seq'=16] {'head'}, dimensions={0} | all-to-all | bytes 5242880 | tf_op jit(solution)/shard_map/all_to_all | solution.py:152
  (225 shorter events, 109.4 us)
Async XLA Ops:
  3.6 4.7 %copy-start.1 = (s32[20,4,64]{2,1,0:T(4,128)S(1)}, s32[20,4,64]{2,1,0:T(4,128)}, u32[]{:S(2)}) copy-start(s32[20,4,64]{2,1,0:T(4,128)} %param.11) | copy-start | bytes 61444
  3.6 9.8 %all-to-all-start = ((bf16[2,256,2560]{2,1,0:T(8,128)(2,1)}), bf16[2,256,2560]{2,1,0:T(8,128)(2,1)S(1)}, u32[]{:S(2)}, u32[]{:S(2)}) async-start(bf16[2,256,2560]{2,1,0:T(8,128)(2,1)} %pad_maximum_fusion), calls=%async_computation | async-start | bytes 5242880 | tf_op jit(solution)/shard_map/all_to_all | solution.py:27
  13.4 1.5 copy-start
  14.9 15.7 %all-to-all-start.1 = ((bf16[256,2,2560]{0,2,1:T(8,128)(2,1)}), bf16[256,2,2560]{0,2,1:T(8,128)(2,1)}, u32[]{:S(2)}, u32[]{:S(2)}) async-start(bf16[256,2,2560]{0,2,1:T(8,128)(2,1)} %bitcast.144), calls=%async_computation.1 | async-start | bytes 5242880 | tf_op jit(solution)/shard_map/all_to_all | solution.py:32
  30.6 20.6 %all-to-all-start.2 = ((bf16[256,2,2560]{0,2,1:T(8,128)(2,1)}), bf16[256,2,2560]{0,2,1:T(8,128)(2,1)S(1)}, u32[]{:S(2)}, u32[]{:S(2)}) async-start(bf16[256,2,2560]{0,2,1:T(8,128)(2,1)} %bitcast.145), calls=%async_computation.2 | async-start | bytes 5242880 | tf_op jit(solution)/shard_map/all_to_all | solution.py:33
  51.2 49.9 %all-to-all-start.3 = ((s32[20,16,4]{0,2,1:T(4,128)}), s32[20,16,4]{0,2,1:T(4,128)S(1)}, u32[]{:S(2)}, u32[]{:S(2)}) async-start(s32[20,16,4]{0,2,1:T(4,128)} %bitcast.11), calls=%async_computation.3 | async-start | bytes 65536 | tf_op jit(solution)/shard_map/all_to_all | solution.py:54
  79.3 2.6 copy-start.2
  106.4 30.7 %all-to-all-start.5 = ((bf16[16,2,128,128]{3,2,1,0:T(8,128)(2,1)}), bf16[16,2,128,128]{3,2,1,0:T(8,128)(2,1)S(1)}, u32[]{:S(2)}, u32[]{:S(2)}) async-start(bf16[16,2,128,128]{3,2,1,0:T(8,128)(2,1)} %copy.61), calls=%async_computation.5 | async-start | bytes 2097152 | tf_op jit(solution)/shard_map/all_to_all | solution.py:132
  137.2 28.9 %all-to-all-start.4 = ((bf16[16,2,128,128]{3,2,1,0:T(8,128)(2,1)}), bf16[16,2,128,128]{3,2,1,0:T(8,128)(2,1)S(1)}, u32[]{:S(2)}, u32[]{:S(2)}) async-start(bf16[16,2,128,128]{3,2,1,0:T(8,128)(2,1)} %copy.60), calls=%async_computation.4 | async-start | bytes 2097152 | tf_op jit(solution)/shard_map/all_to_all | solution.py:131
